TPU v7x, 512 devices: a whole 4x4x16 slice. The times are simulated.
512 devices in a mesh: blk: 128 (over z_lo, y, x), off: 4 (over z_hi, core).
Axes of the slice: x: 4, y: 4, z: 16 (z_hi: 2, z_lo: 8; z = z_hi * 8 + z_lo), core: 2. Of those that a mesh axis runs over, the one named last changes fastest.
Arguments:
- coefficients: bfloat16 [2048, 32, 128], P('blk', 'off'), may hold values from -12 to 12
Outputs:
- smoothed: float32 [2048, 32, 128], P(('blk', 'off'))
- log_degree: float32 [2048], P(('blk', 'off'))
All inputs are finite; a program needn't handle non-finite values.
Results may differ from a plain program's by a relative error of at most 0.005.
Values may be sent and summed in bfloat16 or wider, within the bound.
A program may use at most 64 MiB of HBM per device.

v0:
```python
import math
import jax
import jax.numpy as jnp
from jax import lax
from jax.sharding import PartitionSpec as P

epsilon = 1e-06
concentration = 40.0


def shifted(array, axis, by):
    count = lax.axis_size(axis)
    return lax.ppermute(array, axis, [(i, (i + by) % count) for i in range(count)])


def angle_tables(angular):
    half_width = angular // 2
    frequency = jnp.arange(half_width, dtype=jnp.int32)
    shifts = jnp.arange(angular, dtype=jnp.int32)
    product = frequency[:, None] * shifts[None, :] % angular
    phase = product.astype(jnp.float32) * (2.0 * math.pi / angular)
    forward = jnp.concatenate([jnp.cos(phase), -jnp.sin(phase)], axis=0)
    return (forward, forward.T)


def inverse_norms(block_values):
    values = block_values.astype(jnp.float32)
    return lax.rsqrt(jnp.sum(values * values, axis=(1, 2)) + epsilon)


def tile_terms(own_block, own_inverse, other_block, offset, forward, backward):
    row_count = own_block.shape[0]
    half_width = own_block.shape[2] // 2
    highest = lax.Precision.HIGHEST
    other_inverse = inverse_norms(other_block)
    swapped = jnp.concatenate(
        [other_block[:, :, half_width:], other_block[:, :, :half_width]], axis=2
    )
    direct = jnp.einsum("irc,jrc->ijc", own_block, other_block, preferred_element_type=jnp.float32)
    mixed_terms = jnp.einsum("irc,jrc->ijc", own_block, swapped, preferred_element_type=jnp.float32)
    real_part = direct[:, :, :half_width] + direct[:, :, half_width:]
    imag_part = mixed_terms[:, :, half_width:] - mixed_terms[:, :, :half_width]
    cross_spectrum = jnp.concatenate([real_part, imag_part], axis=2).reshape(
        row_count * row_count, -1
    )
    correlation = jnp.dot(
        cross_spectrum, forward, precision=highest, preferred_element_type=jnp.float32
    )
    correlation = correlation.reshape(row_count, row_count, -1)
    cosine = correlation * own_inverse[:, None, None] * other_inverse[None, :, None]
    same_image = jnp.arange(row_count)[:, None] == jnp.arange(row_count)[None, :]
    keep_mask = jnp.where(jnp.logical_and(offset == 0, same_image), 0.0, 1.0).astype(jnp.float32)
    weights = jnp.exp(concentration * cosine) * keep_mask[:, :, None]
    spectral = jnp.dot(
        weights.reshape(row_count * row_count, -1),
        backward,
        precision=highest,
        preferred_element_type=jnp.float32,
    ).reshape(row_count, row_count, -1)
    degree = jnp.sum(spectral[:, :, 0], axis=1)
    rounded = spectral.astype(jnp.bfloat16)
    weight_real = jnp.concatenate([rounded[:, :, :half_width], rounded[:, :, :half_width]], axis=2)
    weight_imag = jnp.concatenate([-rounded[:, :, half_width:], rounded[:, :, half_width:]], axis=2)
    filtered = jnp.einsum(
        "ijc,jrc->irc", weight_real, other_block, preferred_element_type=jnp.float32
    )
    filtered = filtered + jnp.einsum(
        "ijc,jrc->irc", weight_imag, swapped, preferred_element_type=jnp.float32
    )
    return (filtered, degree)


def body(coefficients):
    own_block = lax.all_gather(coefficients, "off", axis=1, tiled=True)
    own_inverse = inverse_norms(own_block)
    row_count, radial, angular = own_block.shape
    forward, backward = angle_tables(angular)
    ranges = lax.axis_size("off")
    per_range = min(8, lax.axis_size("blk") // ranges)
    range_index = lax.axis_index("off")
    range_base = range_index * per_range
    packet = own_block
    for bit_number in range(ranges.bit_length() - 1):
        moved_packet = shifted(packet, "blk", -(per_range << bit_number))
        chosen = range_index // (1 << bit_number) % 2 == 1
        packet = jnp.where(chosen, moved_packet, packet)
    empty_sum = jnp.zeros((row_count, radial, angular), jnp.float32)
    empty_degree = jnp.zeros((row_count,), jnp.float32)

    def advance_one(step, loop_state):
        filtered, degree, current = loop_state
        terms = tile_terms(own_block, own_inverse, current, range_base + step, forward, backward)
        current = shifted(current, "blk", -1)
        return (filtered + terms[0], degree + terms[1], current)

    last_step = per_range - 1
    filtered, degree, current = lax.fori_loop(
        0, last_step, advance_one, (empty_sum, empty_degree, packet)
    )
    terms = tile_terms(own_block, own_inverse, current, range_base + last_step, forward, backward)
    filtered = filtered + terms[0]
    degree = degree + terms[1]
    totals = (
        lax.psum_scatter(filtered, "off", scatter_dimension=0, tiled=True),
        lax.psum_scatter(degree, "off", scatter_dimension=0, tiled=True),
    )
    smoothed = totals[0] / totals[1][:, None, None]
    return (smoothed, jnp.log(totals[1]))


def solution(mesh):
    return jax.shard_map(
        body,
        mesh=mesh,
        in_specs=(P("blk", "off", None),),
        out_specs=(P(("blk", "off"), None, None), P(("blk", "off"))),
        check_vma=False,
    )
```

profile of v0, /device:TPU:1, one launch (start us, length us, event | category | flops | bytes accessed | tf_op | source)
XLA Modules:
  0.0 278.7 jit_solution(10738338174467296353)
XLA Ops:
  8.2 28.6 %all_gather.3 = bf16[16,32,128]{0,1,2:T(8,128)(2,1)S(1)} all-gather(bf16[16,8,128]{0,1,2:T(8,128)(2,1)S(1)} %copy.20), channel_id=1, replica_groups=mesh['blk'=128,'off'=4] {'off'}, dimensions={1}, use_global_device_ids=true | all-gather | bytes 163840 | tf_op jit(solution)/shard_map/all_gather | solution.py:74
  38.0 14.6 %collective-permute-start.1 = (bf16[16,32,128]{2,1,0:T(8,128)(2,1)S(1)}, bf16[16,32,128]{2,1,0:T(8,128)(2,1)S(1)}, u32[]{:S(2)}, u32[]{:S(2)}) collective-permute-start(bf16[16,32,128]{2,1,0:T(8,128)(2,1)S(1)} %copy.21), channel_id=1, source_target_pairs={{0,480},{4,484},{8,488},{12,492},{16,496},{20,500},{24,504},{28,50... | collective-permute-start | bytes 393224 | tf_op jit(solution)/shard_map/ppermute | solution.py:13
  53.4 1.9 collective-permute-done.1
  55.3 2.4 copy.22
  60.2 9.7 %collective-permute-start.2 = (bf16[16,32,128]{2,1,0:T(8,128)(2,1)S(1)}, bf16[16,32,128]{2,1,0:T(8,128)(2,1)S(1)}, u32[]{:S(2)}, u32[]{:S(2)}) collective-permute-start(bf16[16,32,128]{2,1,0:T(8,128)(2,1)S(1)} %copy.23), channel_id=1, source_target_pairs={{0,448},{4,452},{8,456},{12,460},{16,464},{20,468},{24,472},{28,47... | collective-permute-start | bytes 393224 | tf_op jit(solution)/shard_map/ppermute | solution.py:13
  71.2 1.8 collective-permute-done.2
  75.6 2.5 copy.25
  78.1 125.4 %while.18 = (s32[]{:T(128)}, f32[16,32,128]{1,0,2:T(8,128)}, f32[16]{0:T(128)}, bf16[16,32,128]{2,1,0:T(8,128)(2,1)S(1)}, bf16[16,32,128]{1,0,2:T(8,128)(2,1)S(1...) while((s32[]{:T(128)}, f32[16,32,128]{1,0,2:T(8,128)}, ...), condition=%wide.region_4.5_spmd.clone, body=%wide.region_1.4_spmd.clone.sunk | while | flops 110216208 | bytes 6230326 | solution.py:97
  78.3 16.1 %collective-permute-start = (bf16[16,32,128]{2,1,0:T(8,128)(2,1)S(1)}, bf16[16,32,128]{2,1,0:T(8,128)(2,1)S(1)}, u32[]{:S(2)}, u32[]{:S(2)}) collective-permute-start(bf16[16,32,128]{2,1,0:T(8,128)(2,1)S(1)} %copy.56), channel_id=1, source_target_pairs={{0,508},{4,0},{8,4},{12,8},{16,12},{20,16},{24,20},{28,24},{32,28}... | collective-permute-start | bytes 393224 | tf_op jit(solution)/shard_map/while/body/eval_jaxpr/ppermute | solution.py:13
  102.4 9.1 %collective-permute-start = (bf16[16,32,128]{2,1,0:T(8,128)(2,1)S(1)}, bf16[16,32,128]{2,1,0:T(8,128)(2,1)S(1)}, u32[]{:S(2)}, u32[]{:S(2)}) collective-permute-start(bf16[16,32,128]{2,1,0:T(8,128)(2,1)S(1)} %copy.56), channel_id=1, source_target_pairs={{0,508},{4,0},{8,4},{12,8},{16,12},{20,16},{24,20},{28,24},{32,28}... | collective-permute-start | bytes 393224 | tf_op jit(solution)/shard_map/while/body/eval_jaxpr/ppermute | solution.py:13
  117.5 2.7 fusion.95
  120.8 7.3 %collective-permute-start = (bf16[16,32,128]{2,1,0:T(8,128)(2,1)S(1)}, bf16[16,32,128]{2,1,0:T(8,128)(2,1)S(1)}, u32[]{:S(2)}, u32[]{:S(2)}) collective-permute-start(bf16[16,32,128]{2,1,0:T(8,128)(2,1)S(1)} %copy.56), channel_id=1, source_target_pairs={{0,508},{4,0},{8,4},{12,8},{16,12},{20,16},{24,20},{28,24},{32,28}... | collective-permute-start | bytes 393224 | tf_op jit(solution)/shard_map/while/body/eval_jaxpr/ppermute | solution.py:13
  134.1 2.7 fusion.95
  137.3 7.3 %collective-permute-start = (bf16[16,32,128]{2,1,0:T(8,128)(2,1)S(1)}, bf16[16,32,128]{2,1,0:T(8,128)(2,1)S(1)}, u32[]{:S(2)}, u32[]{:S(2)}) collective-permute-start(bf16[16,32,128]{2,1,0:T(8,128)(2,1)S(1)} %copy.56), channel_id=1, source_target_pairs={{0,508},{4,0},{8,4},{12,8},{16,12},{20,16},{24,20},{28,24},{32,28}... | collective-permute-start | bytes 393224 | tf_op jit(solution)/shard_map/while/body/eval_jaxpr/ppermute | solution.py:13
  150.6 2.7 fusion.95
  153.9 7.3 %collective-permute-start = (bf16[16,32,128]{2,1,0:T(8,128)(2,1)S(1)}, bf16[16,32,128]{2,1,0:T(8,128)(2,1)S(1)}, u32[]{:S(2)}, u32[]{:S(2)}) collective-permute-start(bf16[16,32,128]{2,1,0:T(8,128)(2,1)S(1)} %copy.56), channel_id=1, source_target_pairs={{0,508},{4,0},{8,4},{12,8},{16,12},{20,16},{24,20},{28,24},{32,28}... | collective-permute-start | bytes 393224 | tf_op jit(solution)/shard_map/while/body/eval_jaxpr/ppermute | solution.py:13
  167.2 2.7 fusion.95
  170.5 7.3 %collective-permute-start = (bf16[16,32,128]{2,1,0:T(8,128)(2,1)S(1)}, bf16[16,32,128]{2,1,0:T(8,128)(2,1)S(1)}, u32[]{:S(2)}, u32[]{:S(2)}) collective-permute-start(bf16[16,32,128]{2,1,0:T(8,128)(2,1)S(1)} %copy.56), channel_id=1, source_target_pairs={{0,508},{4,0},{8,4},{12,8},{16,12},{20,16},{24,20},{28,24},{32,28}... | collective-permute-start | bytes 393224 | tf_op jit(solution)/shard_map/while/body/eval_jaxpr/ppermute | solution.py:13
  183.7 2.7 fusion.95
  187.0 7.3 %collective-permute-start = (bf16[16,32,128]{2,1,0:T(8,128)(2,1)S(1)}, bf16[16,32,128]{2,1,0:T(8,128)(2,1)S(1)}, u32[]{:S(2)}, u32[]{:S(2)}) collective-permute-start(bf16[16,32,128]{2,1,0:T(8,128)(2,1)S(1)} %copy.56), channel_id=1, source_target_pairs={{0,508},{4,0},{8,4},{12,8},{16,12},{20,16},{24,20},{28,24},{32,28}... | collective-permute-start | bytes 393224 | tf_op jit(solution)/shard_map/while/body/eval_jaxpr/ppermute | solution.py:13
  200.3 2.7 fusion.95
  210.1 1.6 fusion.17
  215.0 21.4 %all-reduce = f32[16]{0:T(128)S(1)} all-reduce(f32[16]{0:T(128)S(1)} %add.125), channel_id=3, replica_groups=mesh['blk'=128,'off'=4] {'off'}, use_global_device_ids=true, to_apply=%region_8.9.clone | all-reduce | flops 16 | bytes 128
  237.0 33.3 %reduce-scatter.2.cloned.1.call-done = f32[4,32,128]{2,1,0:T(8,128)} async-done(((f32[16,32,128]{2,1,0:T(8,128)}), f32[4,32,128]{2,1,0:T(8,128)}) %reduce-scatter.2.cloned.1.call-update) | async-done | bytes 65552 | tf_op jit(solution)/shard_map/reduce_scatter | solution.py:104
  (256 shorter events, 66.7 us)
Async XLA Ops:
  7.2 263.1 %reduce-scatter.2.cloned.1.call-start = ((), (), s32[]{:S(2)}) async-start(), calls=%async_computation.1 | async-start | bytes 327680 | tf_op jit(solution)/shard_map/reduce_scatter | solution.py:104
  36.8 33.2 %copy-start = (bf16[16,32,128]{0,1,2:T(8,128)(2,1)}, bf16[16,32,128]{0,1,2:T(8,128)(2,1)S(1)}, u32[]{:S(2)}) copy-start(bf16[16,32,128]{0,1,2:T(8,128)(2,1)S(1)} %all_gather.3) | copy-start | bytes 393220
  38.0 17.3 %collective-permute-start.1 = (bf16[16,32,128]{2,1,0:T(8,128)(2,1)S(1)}, bf16[16,32,128]{2,1,0:T(8,128)(2,1)S(1)}, u32[]{:S(2)}, u32[]{:S(2)}) collective-permute-start(bf16[16,32,128]{2,1,0:T(8,128)(2,1)S(1)} %copy.21), channel_id=1, source_target_pairs={{0,480},{4,484},{8,488},{12,492},{16,496},{20,500},{24,504},{28,50... | collective-permute-start | bytes 393224 | tf_op jit(solution)/shard_map/ppermute | solution.py:13
  53.3 16.6 %copy-start.3 = (f32[64,128]{1,0:T(8,128)}, f32[64,128]{1,0:T(8,128)S(1)}, u32[]{:S(2)}) copy-start(f32[64,128]{1,0:T(8,128)S(1)} %get-tuple-element.249) | copy-start | bytes 98308
  53.3 16.6 %copy-start.5 = (f32[64,128]{1,0:T(8,128)}, f32[64,128]{1,0:T(8,128)S(1)}, u32[]{:S(2)}) copy-start(f32[64,128]{1,0:T(8,128)S(1)} %get-tuple-element.250) | copy-start | bytes 98308
  60.2 12.8 %collective-permute-start.2 = (bf16[16,32,128]{2,1,0:T(8,128)(2,1)S(1)}, bf16[16,32,128]{2,1,0:T(8,128)(2,1)S(1)}, u32[]{:S(2)}, u32[]{:S(2)}) collective-permute-start(bf16[16,32,128]{2,1,0:T(8,128)(2,1)S(1)} %copy.23), channel_id=1, source_target_pairs={{0,448},{4,452},{8,456},{12,460},{16,464},{20,468},{24,472},{28,47... | collective-permute-start | bytes 393224 | tf_op jit(solution)/shard_map/ppermute | solution.py:13
  78.3 23.6 %collective-permute-start = (bf16[16,32,128]{2,1,0:T(8,128)(2,1)S(1)}, bf16[16,32,128]{2,1,0:T(8,128)(2,1)S(1)}, u32[]{:S(2)}, u32[]{:S(2)}) collective-permute-start(bf16[16,32,128]{2,1,0:T(8,128)(2,1)S(1)} %copy.56), channel_id=1, source_target_pairs={{0,508},{4,0},{8,4},{12,8},{16,12},{20,16},{24,20},{28,24},{32,28}... | collective-permute-start | bytes 393224 | tf_op jit(solution)/shard_map/while/body/eval_jaxpr/ppermute | solution.py:13
  100.4 1.5 copy-start.7
  102.4 17.8 %collective-permute-start = (bf16[16,32,128]{2,1,0:T(8,128)(2,1)S(1)}, bf16[16,32,128]{2,1,0:T(8,128)(2,1)S(1)}, u32[]{:S(2)}, u32[]{:S(2)}) collective-permute-start(bf16[16,32,128]{2,1,0:T(8,128)(2,1)S(1)} %copy.56), channel_id=1, source_target_pairs={{0,508},{4,0},{8,4},{12,8},{16,12},{20,16},{24,20},{28,24},{32,28}... | collective-permute-start | bytes 393224 | tf_op jit(solution)/shard_map/while/body/eval_jaxpr/ppermute | solution.py:13
  117.5 2.7 copy-start.7
  120.8 16.0 %collective-permute-start = (bf16[16,32,128]{2,1,0:T(8,128)(2,1)S(1)}, bf16[16,32,128]{2,1,0:T(8,128)(2,1)S(1)}, u32[]{:S(2)}, u32[]{:S(2)}) collective-permute-start(bf16[16,32,128]{2,1,0:T(8,128)(2,1)S(1)} %copy.56), channel_id=1, source_target_pairs={{0,508},{4,0},{8,4},{12,8},{16,12},{20,16},{24,20},{28,24},{32,28}... | collective-permute-start | bytes 393224 | tf_op jit(solution)/shard_map/while/body/eval_jaxpr/ppermute | solution.py:13
  134.1 2.7 copy-start.7
  137.3 16.0 %collective-permute-start = (bf16[16,32,128]{2,1,0:T(8,128)(2,1)S(1)}, bf16[16,32,128]{2,1,0:T(8,128)(2,1)S(1)}, u32[]{:S(2)}, u32[]{:S(2)}) collective-permute-start(bf16[16,32,128]{2,1,0:T(8,128)(2,1)S(1)} %copy.56), channel_id=1, source_target_pairs={{0,508},{4,0},{8,4},{12,8},{16,12},{20,16},{24,20},{28,24},{32,28}... | collective-permute-start | bytes 393224 | tf_op jit(solution)/shard_map/while/body/eval_jaxpr/ppermute | solution.py:13
  150.6 2.7 copy-start.7
  153.9 16.0 %collective-permute-start = (bf16[16,32,128]{2,1,0:T(8,128)(2,1)S(1)}, bf16[16,32,128]{2,1,0:T(8,128)(2,1)S(1)}, u32[]{:S(2)}, u32[]{:S(2)}) collective-permute-start(bf16[16,32,128]{2,1,0:T(8,128)(2,1)S(1)} %copy.56), channel_id=1, source_target_pairs={{0,508},{4,0},{8,4},{12,8},{16,12},{20,16},{24,20},{28,24},{32,28}... | collective-permute-start | bytes 393224 | tf_op jit(solution)/shard_map/while/body/eval_jaxpr/ppermute | solution.py:13
  167.2 2.7 copy-start.7
  170.5 16.0 %collective-permute-start = (bf16[16,32,128]{2,1,0:T(8,128)(2,1)S(1)}, bf16[16,32,128]{2,1,0:T(8,128)(2,1)S(1)}, u32[]{:S(2)}, u32[]{:S(2)}) collective-permute-start(bf16[16,32,128]{2,1,0:T(8,128)(2,1)S(1)} %copy.56), channel_id=1, source_target_pairs={{0,508},{4,0},{8,4},{12,8},{16,12},{20,16},{24,20},{28,24},{32,28}... | collective-permute-start | bytes 393224 | tf_op jit(solution)/shard_map/while/body/eval_jaxpr/ppermute | solution.py:13
  183.7 2.7 copy-start.7
  187.0 16.0 %collective-permute-start = (bf16[16,32,128]{2,1,0:T(8,128)(2,1)S(1)}, bf16[16,32,128]{2,1,0:T(8,128)(2,1)S(1)}, u32[]{:S(2)}, u32[]{:S(2)}) collective-permute-start(bf16[16,32,128]{2,1,0:T(8,128)(2,1)S(1)} %copy.56), channel_id=1, source_target_pairs={{0,508},{4,0},{8,4},{12,8},{16,12},{20,16},{24,20},{28,24},{32,28}... | collective-permute-start | bytes 393224 | tf_op jit(solution)/shard_map/while/body/eval_jaxpr/ppermute | solution.py:13
  200.3 2.7 copy-start.7
  203.7 1.2 copy-start.1
  206.2 0.8 copy-start.6
  208.2 1.9 copy-start.2
  211.7 3.3 %copy-start.9 = (f32[16]{0:T(128)S(1)}, f32[16]{0:T(128)}, u32[]{:S(2)}) copy-start(f32[16]{0:T(128)} %get-tuple-element.160) | copy-start | bytes 196
  (8 other events, 4.8 us)
Sparse Core Ops, SparseCore 0:
  213.0 57.2 reduce-scatter.1
where the time goes:
time: 280 us; the launch traced here: 279 us
  starting transfers between devices  86.1 us (31%)
  blocking collectives  50 us (18%)
  matrix products  40.1 us (14%)
  local copies, waits for them, and re-layouts  37.3 us (13%)
  waiting for transfers between devices  37.1 us (13%)
  between operations  15 us (5%)
  other arithmetic  11.9 us (4%)
    ppermute x9, starting transfers between devices, shifted(): lax.ppermute(array, axis, [(i, (i + by) % count) for i in range(count)])  86.1 us
    reduce_scatter x1, waiting for transfers between devices, body(): lax.psum_scatter(filtered, 'off', scatter_dimension=0, tiled=True)  33.3 us
    all_gather x1, blocking collectives, body(): own_block = lax.all_gather(coefficients, 'off', axis=1, tiled=True)  28.6 us
    unnamed x1, blocking collectives  21.4 us
    dot_general x8, matrix products, tile_terms(): jnp.einsum('ijc,jrc->irc', weight_imag, swapped, preferred_element_type=j...  19.2 us
    dot_general x8, matrix products, tile_terms(): jnp.dot(weights.reshape(row_count * row_count, -1), backward, precision=h...  7.98 us
    while x42, local copies, waits for them, and re-layouts  7.01 us
    unnamed x21, local copies, waits for them, and re-layouts  6.46 us
  transfers between devices with their start and end apart: 10, of which 3 were waited for; matrix products, arithmetic and copies ran while one was open for 22% of the time, Pallas kernels for 0%

commit v1 on v0

--- a/solution.py
+++ b/solution.py
@@ -71,7 +71,7 @@
 
 
 def body(coefficients):
-    own_block = lax.all_gather(coefficients, "off", axis=1, tiled=True)
+    own_block = jnp.concatenate(lax.all_gather(coefficients, "off"), axis=1)
     own_inverse = inverse_norms(own_block)
     row_count, radial, angular = own_block.shape
     forward, backward = angle_tables(angular)

time: 280 us -> 250 us (0.89)
  matrix products: 40.1 us -> 32 us
  blocking collectives: 50 us -> 44 us
  local copies, waits for them, and re-layouts: 37.3 us -> 32.2 us
  starting transfers between devices: 86.1 us -> 81.9 us
  waiting for transfers between devices: 37.1 us -> 33.7 us
    all_gather x1, blocking collectives: 28.6 us -> 21 us  [body(): own_block = jnp.concatenate(lax.all_gather(coefficients, 'off'), axis=1)]
    dot_general x8, matrix products: 7.98 us -> 2.11 us  [tile_terms(): jnp.dot(weights.reshape(row_count * row_count, -1), backward, precision=h...]
    ppermute x9, starting transfers between devices: 86.1 us -> 81.9 us  [shifted(): lax.ppermute(array, axis, [(i, (i + by) % count) for i in range(count)])]
    reduce_scatter x1, waiting for transfers between devices: 33.3 us -> 29.3 us  [body(): lax.psum_scatter(filtered, 'off', scatter_dimension=0, tiled=True)]
    ppermute x2 -> x0, local copies, waits for them, and re-layouts: 3.87 us -> none  [shifted(): lax.ppermute(array, axis, [(i, (i + by) % count) for i in range(count)])]
    while x42 -> x70, local copies, waits for them, and re-layouts: 7.01 us -> 10.8 us
    unnamed x21 -> x15, local copies, waits for them, and re-layouts: 6.46 us -> 3.68 us
where the time goes in v1:
time: 250 us; the launch traced here: 249 us
  starting transfers between devices  81.9 us (33%)
  blocking collectives  44 us (18%)
  waiting for transfers between devices  33.7 us (13%)
  local copies, waits for them, and re-layouts  32.2 us (13%)
  matrix products  32 us (13%)
  between operations  15 us (6%)
  other arithmetic  9.28 us (4%)
    ppermute x9, starting transfers between devices, shifted(): lax.ppermute(array, axis, [(i, (i + by) % count) for i in range(count)])  81.9 us
    reduce_scatter x1, waiting for transfers between devices, body(): lax.psum_scatter(filtered, 'off', scatter_dimension=0, tiled=True)  29.3 us
    unnamed x1, blocking collectives  23 us
    all_gather x1, blocking collectives, body(): own_block = jnp.concatenate(lax.all_gather(coefficients, 'off'), axis=1)  21 us
    dot_general x8, matrix products, tile_terms(): jnp.einsum('ijc,jrc->irc', weight_imag, swapped, preferred_element_type=j...  17.8 us
    while x70, local copies, waits for them, and re-layouts  10.8 us
  transfers between devices with their start and end apart: 10, of which 3 were waited for; matrix products, arithmetic and copies ran while one was open for 22% of the time, Pallas kernels for 0%

profile of v1, /device:TPU:1, one launch (start us, length us, event | category | flops | bytes accessed | tf_op | source)
XLA Modules:
  0.0 249.0 jit_solution(8697174802594981260)
XLA Ops:
  7.2 21.0 %all-gather = bf16[64,8,128]{2,1,0:T(8,128)(2,1)S(1)} all-gather(bf16[16,8,128]{2,1,0:T(8,128)(2,1)} %param.3), channel_id=2, replica_groups=mesh['blk'=128,'off'=4] {'off'}, dimensions={0}, use_global_device_ids=true | all-gather | bytes 163840 | tf_op jit(solution)/shard_map/all_gather | solution.py:74
  28.3 10.2 %collective-permute-start.1 = (bf16[16,32,128]{2,1,0:T(8,128)(2,1)S(1)}, bf16[16,32,128]{2,1,0:T(8,128)(2,1)S(1)}, u32[]{:S(2)}, u32[]{:S(2)}) collective-permute-start(bf16[16,32,128]{2,1,0:T(8,128)(2,1)S(1)} %copy_bitcast_fusion), channel_id=1, source_target_pairs={{0,480},{4,484},{8,488},{12,492},{16,496},{20,500},{24,504},{28,50... | collective-permute-start | bytes 393224 | tf_op jit(solution)/shard_map/ppermute | solution.py:13
  38.8 2.3 collective-permute-done.1
  41.1 3.0 %collective-permute-start.2 = (bf16[16,32,128]{2,1,0:T(8,128)(2,1)S(1)}, bf16[16,32,128]{2,1,0:T(8,128)(2,1)S(1)}, u32[]{:S(2)}, u32[]{:S(2)}) collective-permute-start(bf16[16,32,128]{2,1,0:T(8,128)(2,1)S(1)} %broadcast_select_fusion.1), channel_id=1, source_target_pairs={{0,448},{4,452},{8,456},{12,460},{16,464},{20,468},{24,472},{28,47... | collective-permute-start | bytes 393224 | tf_op jit(solution)/shard_map/ppermute | solution.py:13
  44.8 2.1 collective-permute-done.2
  46.9 130.2 %while.18 = (s32[]{:T(128)}, f32[16,32,128]{1,0,2:T(8,128)}, f32[16]{0:T(128)}, bf16[16,32,128]{2,1,0:T(8,128)(2,1)S(1)}, bf16[16,32,128]{1,0,2:T(8,128)(2,1)S(1...) while((s32[]{:T(128)}, f32[16,32,128]{1,0,2:T(8,128)}, ...), condition=%wide.region_4.5_spmd.clone, body=%wide.region_1.4_spmd.clone.sunk | while | flops 110216208 | bytes 6754670 | solution.py:97
  46.9 21.7 %collective-permute-start = (bf16[16,32,128]{2,1,0:T(8,128)(2,1)S(1)}, bf16[16,32,128]{2,1,0:T(8,128)(2,1)S(1)}, u32[]{:S(2)}, u32[]{:S(2)}) collective-permute-start(bf16[16,32,128]{2,1,0:T(8,128)(2,1)S(1)} %copy.77), channel_id=1, source_target_pairs={{0,508},{4,0},{8,4},{12,8},{16,12},{20,16},{24,20},{28,24},{32,28}... | collective-permute-start | bytes 393224 | tf_op jit(solution)/shard_map/while/body/eval_jaxpr/ppermute | solution.py:13
  73.8 1.4 fusion.96
  76.3 8.9 %collective-permute-start = (bf16[16,32,128]{2,1,0:T(8,128)(2,1)S(1)}, bf16[16,32,128]{2,1,0:T(8,128)(2,1)S(1)}, u32[]{:S(2)}, u32[]{:S(2)}) collective-permute-start(bf16[16,32,128]{2,1,0:T(8,128)(2,1)S(1)} %copy.77), channel_id=1, source_target_pairs={{0,508},{4,0},{8,4},{12,8},{16,12},{20,16},{24,20},{28,24},{32,28}... | collective-permute-start | bytes 393224 | tf_op jit(solution)/shard_map/while/body/eval_jaxpr/ppermute | solution.py:13
  90.4 2.7 %fusion.96 = f32[16,32,128]{1,0,2:T(8,128)} fusion(f32[16,32,128]{1,0,2:T(8,128)S(1)} %convolution_bitcast_fusion.11, bf16[16,16,128]{1,0,2:T(8,128)(2,1)S(1)} %copy.69, bf16[16,32,128]{1,0,2:T(8,128)(2,1)S(1)} %copy.64, f32[16,32,128]{1,0,2:T(8,128)} %get-tuple-element.358, pred[]{:T(512)S(6)} %compare.9), kind=kOutput, calls=%fused_computation.2.clone.1 | convolution fusion | flops 2293760 | bytes 983041 | tf_op jit(solution)/shard_map/while/body/eval_jaxpr/ijc,jrc->irc/dot_general | solution.py:67
  94.2 7.6 %collective-permute-start = (bf16[16,32,128]{2,1,0:T(8,128)(2,1)S(1)}, bf16[16,32,128]{2,1,0:T(8,128)(2,1)S(1)}, u32[]{:S(2)}, u32[]{:S(2)}) collective-permute-start(bf16[16,32,128]{2,1,0:T(8,128)(2,1)S(1)} %copy.77), channel_id=1, source_target_pairs={{0,508},{4,0},{8,4},{12,8},{16,12},{20,16},{24,20},{28,24},{32,28}... | collective-permute-start | bytes 393224 | tf_op jit(solution)/shard_map/while/body/eval_jaxpr/ppermute | solution.py:13
  106.9 2.7 %fusion.96 = f32[16,32,128]{1,0,2:T(8,128)} fusion(f32[16,32,128]{1,0,2:T(8,128)S(1)} %convolution_bitcast_fusion.11, bf16[16,16,128]{1,0,2:T(8,128)(2,1)S(1)} %copy.69, bf16[16,32,128]{1,0,2:T(8,128)(2,1)S(1)} %copy.64, f32[16,32,128]{1,0,2:T(8,128)} %get-tuple-element.358, pred[]{:T(512)S(6)} %compare.9), kind=kOutput, calls=%fused_computation.2.clone.1 | convolution fusion | flops 2293760 | bytes 983041 | tf_op jit(solution)/shard_map/while/body/eval_jaxpr/ijc,jrc->irc/dot_general | solution.py:67
  110.7 7.6 %collective-permute-start = (bf16[16,32,128]{2,1,0:T(8,128)(2,1)S(1)}, bf16[16,32,128]{2,1,0:T(8,128)(2,1)S(1)}, u32[]{:S(2)}, u32[]{:S(2)}) collective-permute-start(bf16[16,32,128]{2,1,0:T(8,128)(2,1)S(1)} %copy.77), channel_id=1, source_target_pairs={{0,508},{4,0},{8,4},{12,8},{16,12},{20,16},{24,20},{28,24},{32,28}... | collective-permute-start | bytes 393224 | tf_op jit(solution)/shard_map/while/body/eval_jaxpr/ppermute | solution.py:13
  123.5 2.7 %fusion.96 = f32[16,32,128]{1,0,2:T(8,128)} fusion(f32[16,32,128]{1,0,2:T(8,128)S(1)} %convolution_bitcast_fusion.11, bf16[16,16,128]{1,0,2:T(8,128)(2,1)S(1)} %copy.69, bf16[16,32,128]{1,0,2:T(8,128)(2,1)S(1)} %copy.64, f32[16,32,128]{1,0,2:T(8,128)} %get-tuple-element.358, pred[]{:T(512)S(6)} %compare.9), kind=kOutput, calls=%fused_computation.2.clone.1 | convolution fusion | flops 2293760 | bytes 983041 | tf_op jit(solution)/shard_map/while/body/eval_jaxpr/ijc,jrc->irc/dot_general | solution.py:67
  127.3 7.6 %collective-permute-start = (bf16[16,32,128]{2,1,0:T(8,128)(2,1)S(1)}, bf16[16,32,128]{2,1,0:T(8,128)(2,1)S(1)}, u32[]{:S(2)}, u32[]{:S(2)}) collective-permute-start(bf16[16,32,128]{2,1,0:T(8,128)(2,1)S(1)} %copy.77), channel_id=1, source_target_pairs={{0,508},{4,0},{8,4},{12,8},{16,12},{20,16},{24,20},{28,24},{32,28}... | collective-permute-start | bytes 393224 | tf_op jit(solution)/shard_map/while/body/eval_jaxpr/ppermute | solution.py:13
  140.0 2.7 %fusion.96 = f32[16,32,128]{1,0,2:T(8,128)} fusion(f32[16,32,128]{1,0,2:T(8,128)S(1)} %convolution_bitcast_fusion.11, bf16[16,16,128]{1,0,2:T(8,128)(2,1)S(1)} %copy.69, bf16[16,32,128]{1,0,2:T(8,128)(2,1)S(1)} %copy.64, f32[16,32,128]{1,0,2:T(8,128)} %get-tuple-element.358, pred[]{:T(512)S(6)} %compare.9), kind=kOutput, calls=%fused_computation.2.clone.1 | convolution fusion | flops 2293760 | bytes 983041 | tf_op jit(solution)/shard_map/while/body/eval_jaxpr/ijc,jrc->irc/dot_general | solution.py:67
  143.8 7.6 %collective-permute-start = (bf16[16,32,128]{2,1,0:T(8,128)(2,1)S(1)}, bf16[16,32,128]{2,1,0:T(8,128)(2,1)S(1)}, u32[]{:S(2)}, u32[]{:S(2)}) collective-permute-start(bf16[16,32,128]{2,1,0:T(8,128)(2,1)S(1)} %copy.77), channel_id=1, source_target_pairs={{0,508},{4,0},{8,4},{12,8},{16,12},{20,16},{24,20},{28,24},{32,28}... | collective-permute-start | bytes 393224 | tf_op jit(solution)/shard_map/while/body/eval_jaxpr/ppermute | solution.py:13
  156.6 2.7 %fusion.96 = f32[16,32,128]{1,0,2:T(8,128)} fusion(f32[16,32,128]{1,0,2:T(8,128)S(1)} %convolution_bitcast_fusion.11, bf16[16,16,128]{1,0,2:T(8,128)(2,1)S(1)} %copy.69, bf16[16,32,128]{1,0,2:T(8,128)(2,1)S(1)} %copy.64, f32[16,32,128]{1,0,2:T(8,128)} %get-tuple-element.358, pred[]{:T(512)S(6)} %compare.9), kind=kOutput, calls=%fused_computation.2.clone.1 | convolution fusion | flops 2293760 | bytes 983041 | tf_op jit(solution)/shard_map/while/body/eval_jaxpr/ijc,jrc->irc/dot_general | solution.py:67
  160.4 7.7 %collective-permute-start = (bf16[16,32,128]{2,1,0:T(8,128)(2,1)S(1)}, bf16[16,32,128]{2,1,0:T(8,128)(2,1)S(1)}, u32[]{:S(2)}, u32[]{:S(2)}) collective-permute-start(bf16[16,32,128]{2,1,0:T(8,128)(2,1)S(1)} %copy.77), channel_id=1, source_target_pairs={{0,508},{4,0},{8,4},{12,8},{16,12},{20,16},{24,20},{28,24},{32,28}... | collective-permute-start | bytes 393224 | tf_op jit(solution)/shard_map/while/body/eval_jaxpr/ppermute | solution.py:13
  173.3 2.7 %fusion.96 = f32[16,32,128]{1,0,2:T(8,128)} fusion(f32[16,32,128]{1,0,2:T(8,128)S(1)} %convolution_bitcast_fusion.11, bf16[16,16,128]{1,0,2:T(8,128)(2,1)S(1)} %copy.69, bf16[16,32,128]{1,0,2:T(8,128)(2,1)S(1)} %copy.64, f32[16,32,128]{1,0,2:T(8,128)} %get-tuple-element.358, pred[]{:T(512)S(6)} %compare.9), kind=kOutput, calls=%fused_computation.2.clone.1 | convolution fusion | flops 2293760 | bytes 983041 | tf_op jit(solution)/shard_map/while/body/eval_jaxpr/ijc,jrc->irc/dot_general | solution.py:67
  185.1 1.3 dynamic-slice
  187.8 23.0 %all-reduce = f32[16]{0:T(128)S(1)} all-reduce(f32[16]{0:T(128)S(1)} %add.125), channel_id=4, replica_groups=mesh['blk'=128,'off'=4] {'off'}, use_global_device_ids=true, to_apply=%region_8.9.clone | all-reduce | flops 16 | bytes 128
  211.4 29.3 %reduce-scatter.2.cloned.1.call-done = f32[4,32,128]{2,1,0:T(8,128)} async-done(((f32[16,32,128]{2,1,0:T(8,128)}), f32[4,32,128]{2,1,0:T(8,128)}) %reduce-scatter.2.cloned.1.call-update) | async-done | bytes 65552 | tf_op jit(solution)/shard_map/reduce_scatter | solution.py:104
  240.6 1.5 broadcast_divide_fusion
  (276 shorter events, 53.2 us)
Async XLA Ops:
  7.2 233.5 %reduce-scatter.2.cloned.1.call-start = ((), (), s32[]{:S(2)}) async-start(), calls=%async_computation.1 | async-start | bytes 327680 | tf_op jit(solution)/shard_map/reduce_scatter | solution.py:104
  28.3 12.8 %collective-permute-start.1 = (bf16[16,32,128]{2,1,0:T(8,128)(2,1)S(1)}, bf16[16,32,128]{2,1,0:T(8,128)(2,1)S(1)}, u32[]{:S(2)}, u32[]{:S(2)}) collective-permute-start(bf16[16,32,128]{2,1,0:T(8,128)(2,1)S(1)} %copy_bitcast_fusion), channel_id=1, source_target_pairs={{0,480},{4,484},{8,488},{12,492},{16,496},{20,500},{24,504},{28,50... | collective-permute-start | bytes 393224 | tf_op jit(solution)/shard_map/ppermute | solution.py:13
  38.8 5.3 %copy-start.3 = (f32[64,128]{1,0:T(8,128)}, f32[64,128]{1,0:T(8,128)S(1)}, u32[]{:S(2)}) copy-start(f32[64,128]{1,0:T(8,128)S(1)} %get-tuple-element.271) | copy-start | bytes 98308
  38.8 5.3 %copy-start.5 = (f32[64,128]{1,0:T(8,128)}, f32[64,128]{1,0:T(8,128)S(1)}, u32[]{:S(2)}) copy-start(f32[64,128]{1,0:T(8,128)S(1)} %get-tuple-element.272) | copy-start | bytes 98308
  41.1 5.7 %collective-permute-start.2 = (bf16[16,32,128]{2,1,0:T(8,128)(2,1)S(1)}, bf16[16,32,128]{2,1,0:T(8,128)(2,1)S(1)}, u32[]{:S(2)}, u32[]{:S(2)}) collective-permute-start(bf16[16,32,128]{2,1,0:T(8,128)(2,1)S(1)} %broadcast_select_fusion.1), channel_id=1, source_target_pairs={{0,448},{4,452},{8,456},{12,460},{16,464},{20,468},{24,472},{28,47... | collective-permute-start | bytes 393224 | tf_op jit(solution)/shard_map/ppermute | solution.py:13
  46.9 24.9 %copy-start.1 = (f32[128,128]{1,0:T(8,128)}, f32[128,128]{1,0:T(8,128)S(1)}, u32[]{:S(2)}) copy-start(f32[128,128]{1,0:T(8,128)S(1)} %get-tuple-element.376) | copy-start | bytes 196612 | tf_op jit(solution)/shard_map/while
  46.9 28.9 %collective-permute-start = (bf16[16,32,128]{2,1,0:T(8,128)(2,1)S(1)}, bf16[16,32,128]{2,1,0:T(8,128)(2,1)S(1)}, u32[]{:S(2)}, u32[]{:S(2)}) collective-permute-start(bf16[16,32,128]{2,1,0:T(8,128)(2,1)S(1)} %copy.77), channel_id=1, source_target_pairs={{0,508},{4,0},{8,4},{12,8},{16,12},{20,16},{24,20},{28,24},{32,28}... | collective-permute-start | bytes 393224 | tf_op jit(solution)/shard_map/while/body/eval_jaxpr/ppermute | solution.py:13
  76.3 12.1 %copy-start.1 = (f32[128,128]{1,0:T(8,128)}, f32[128,128]{1,0:T(8,128)S(1)}, u32[]{:S(2)}) copy-start(f32[128,128]{1,0:T(8,128)S(1)} %get-tuple-element.376) | copy-start | bytes 196612 | tf_op jit(solution)/shard_map/while
  76.3 17.3 %collective-permute-start = (bf16[16,32,128]{2,1,0:T(8,128)(2,1)S(1)}, bf16[16,32,128]{2,1,0:T(8,128)(2,1)S(1)}, u32[]{:S(2)}, u32[]{:S(2)}) collective-permute-start(bf16[16,32,128]{2,1,0:T(8,128)(2,1)S(1)} %copy.77), channel_id=1, source_target_pairs={{0,508},{4,0},{8,4},{12,8},{16,12},{20,16},{24,20},{28,24},{32,28}... | collective-permute-start | bytes 393224 | tf_op jit(solution)/shard_map/while/body/eval_jaxpr/ppermute | solution.py:13
  90.4 3.8 %copy-start.2 = (f32[128,128]{1,0:T(8,128)S(1)}, f32[128,128]{1,0:T(8,128)}, u32[]{:S(2)}) copy-start(f32[128,128]{1,0:T(8,128)} %copy-done.1) | copy-start | bytes 196612 | tf_op jit(solution)/shard_map/while
  94.1 10.8 %copy-start.1 = (f32[128,128]{1,0:T(8,128)}, f32[128,128]{1,0:T(8,128)S(1)}, u32[]{:S(2)}) copy-start(f32[128,128]{1,0:T(8,128)S(1)} %get-tuple-element.376) | copy-start | bytes 196612 | tf_op jit(solution)/shard_map/while
  94.2 16.0 %collective-permute-start = (bf16[16,32,128]{2,1,0:T(8,128)(2,1)S(1)}, bf16[16,32,128]{2,1,0:T(8,128)(2,1)S(1)}, u32[]{:S(2)}, u32[]{:S(2)}) collective-permute-start(bf16[16,32,128]{2,1,0:T(8,128)(2,1)S(1)} %copy.77), channel_id=1, source_target_pairs={{0,508},{4,0},{8,4},{12,8},{16,12},{20,16},{24,20},{28,24},{32,28}... | collective-permute-start | bytes 393224 | tf_op jit(solution)/shard_map/while/body/eval_jaxpr/ppermute | solution.py:13
  106.9 3.8 %copy-start.2 = (f32[128,128]{1,0:T(8,128)S(1)}, f32[128,128]{1,0:T(8,128)}, u32[]{:S(2)}) copy-start(f32[128,128]{1,0:T(8,128)} %copy-done.1) | copy-start | bytes 196612 | tf_op jit(solution)/shard_map/while
  110.7 10.8 %copy-start.1 = (f32[128,128]{1,0:T(8,128)}, f32[128,128]{1,0:T(8,128)S(1)}, u32[]{:S(2)}) copy-start(f32[128,128]{1,0:T(8,128)S(1)} %get-tuple-element.376) | copy-start | bytes 196612 | tf_op jit(solution)/shard_map/while
  110.7 16.0 %collective-permute-start = (bf16[16,32,128]{2,1,0:T(8,128)(2,1)S(1)}, bf16[16,32,128]{2,1,0:T(8,128)(2,1)S(1)}, u32[]{:S(2)}, u32[]{:S(2)}) collective-permute-start(bf16[16,32,128]{2,1,0:T(8,128)(2,1)S(1)} %copy.77), channel_id=1, source_target_pairs={{0,508},{4,0},{8,4},{12,8},{16,12},{20,16},{24,20},{28,24},{32,28}... | collective-permute-start | bytes 393224 | tf_op jit(solution)/shard_map/while/body/eval_jaxpr/ppermute | solution.py:13
  123.5 3.8 %copy-start.2 = (f32[128,128]{1,0:T(8,128)S(1)}, f32[128,128]{1,0:T(8,128)}, u32[]{:S(2)}) copy-start(f32[128,128]{1,0:T(8,128)} %copy-done.1) | copy-start | bytes 196612 | tf_op jit(solution)/shard_map/while
  127.3 10.8 %copy-start.1 = (f32[128,128]{1,0:T(8,128)}, f32[128,128]{1,0:T(8,128)S(1)}, u32[]{:S(2)}) copy-start(f32[128,128]{1,0:T(8,128)S(1)} %get-tuple-element.376) | copy-start | bytes 196612 | tf_op jit(solution)/shard_map/while
  127.3 16.0 %collective-permute-start = (bf16[16,32,128]{2,1,0:T(8,128)(2,1)S(1)}, bf16[16,32,128]{2,1,0:T(8,128)(2,1)S(1)}, u32[]{:S(2)}, u32[]{:S(2)}) collective-permute-start(bf16[16,32,128]{2,1,0:T(8,128)(2,1)S(1)} %copy.77), channel_id=1, source_target_pairs={{0,508},{4,0},{8,4},{12,8},{16,12},{20,16},{24,20},{28,24},{32,28}... | collective-permute-start | bytes 393224 | tf_op jit(solution)/shard_map/while/body/eval_jaxpr/ppermute | solution.py:13
  143.8 10.8 %copy-start.1 = (f32[128,128]{1,0:T(8,128)}, f32[128,128]{1,0:T(8,128)S(1)}, u32[]{:S(2)}) copy-start(f32[128,128]{1,0:T(8,128)S(1)} %get-tuple-element.376) | copy-start | bytes 196612 | tf_op jit(solution)/shard_map/while
  143.8 16.0 %collective-permute-start = (bf16[16,32,128]{2,1,0:T(8,128)(2,1)S(1)}, bf16[16,32,128]{2,1,0:T(8,128)(2,1)S(1)}, u32[]{:S(2)}, u32[]{:S(2)}) collective-permute-start(bf16[16,32,128]{2,1,0:T(8,128)(2,1)S(1)} %copy.77), channel_id=1, source_target_pairs={{0,508},{4,0},{8,4},{12,8},{16,12},{20,16},{24,20},{28,24},{32,28}... | collective-permute-start | bytes 393224 | tf_op jit(solution)/shard_map/while/body/eval_jaxpr/ppermute | solution.py:13
  156.6 3.8 %copy-start.2 = (f32[128,128]{1,0:T(8,128)S(1)}, f32[128,128]{1,0:T(8,128)}, u32[]{:S(2)}) copy-start(f32[128,128]{1,0:T(8,128)} %copy-done.1) | copy-start | bytes 196612 | tf_op jit(solution)/shard_map/while
  160.4 10.9 %copy-start.1 = (f32[128,128]{1,0:T(8,128)}, f32[128,128]{1,0:T(8,128)S(1)}, u32[]{:S(2)}) copy-start(f32[128,128]{1,0:T(8,128)S(1)} %get-tuple-element.376) | copy-start | bytes 196612 | tf_op jit(solution)/shard_map/while
  160.4 16.2 %collective-permute-start = (bf16[16,32,128]{2,1,0:T(8,128)(2,1)S(1)}, bf16[16,32,128]{2,1,0:T(8,128)(2,1)S(1)}, u32[]{:S(2)}, u32[]{:S(2)}) collective-permute-start(bf16[16,32,128]{2,1,0:T(8,128)(2,1)S(1)} %copy.77), channel_id=1, source_target_pairs={{0,508},{4,0},{8,4},{12,8},{16,12},{20,16},{24,20},{28,24},{32,28}... | collective-permute-start | bytes 393224 | tf_op jit(solution)/shard_map/while/body/eval_jaxpr/ppermute | solution.py:13
  173.2 3.8 %copy-start.2 = (f32[128,128]{1,0:T(8,128)S(1)}, f32[128,128]{1,0:T(8,128)}, u32[]{:S(2)}) copy-start(f32[128,128]{1,0:T(8,128)} %copy-done.1) | copy-start | bytes 196612 | tf_op jit(solution)/shard_map/while
  (20 other events, 17.3 us)
Sparse Core Ops, SparseCore 0:
  185.2 55.4 reduce-scatter.1
